TPU v7x, 32 devices: a whole 2x2x4 slice. The times are simulated.
32 devices in a mesh: occ: 8 (over z, x), aux: 4 (over y, core).
Axes of the slice: x: 2, y: 2, z: 4, core: 2. Of those that a mesh axis runs over, the one named last changes fastest.
Arguments:
- three_index: bfloat16 [8, 448, 1536], P('occ', None, 'aux'), may hold values from -0.75 to 0.75
- occ_energy: float32 [8], P('occ'), may hold values from -2 to -0.3
- vir_energy: float32 [448], replicated, may hold values from 0.3 to 3
Outputs:
- gamma: float32 [8, 448, 1536], P('occ', None, 'aux')
All inputs are finite; a program needn't handle non-finite values.
Results may differ from a plain program's by a relative error of at most 0.0019.
Values may be sent and summed in bfloat16 or wider, within the bound.
A program may use at most 64 MiB of HBM per device.

v0:
```python
import jax
import jax.numpy as jnp
from jax import lax
from jax.sharding import PartitionSpec as P


def from_behind(array, axis, by):
    size = lax.axis_size(axis)
    return lax.ppermute(array, axis, [(i, (i + by) % size) for i in range(size)])


def pair_amps(rows_i, eps_i, rows_j, eps_j, vir_energy):
    partial_value = lax.dot_general(
        rows_i, rows_j, (((1,), (1,)), ((), ())), preferred_element_type=jnp.float32
    )
    occ_count = eps_i.shape[0]
    vir_count = vir_energy.shape[0]
    width = occ_count * vir_count
    four = partial_value.reshape(occ_count, vir_count, occ_count, vir_count)
    numer = (2.0 * four - jnp.transpose(four, (0, 3, 2, 1))).reshape(width, width)
    denom = (
        vir_energy[None, :, None, None]
        + vir_energy[None, None, None, :]
        - eps_i[:, None, None, None]
        - eps_j[None, None, :, None]
    ).reshape(width, width)
    share = width // lax.axis_size("aux")
    mine = lax.psum_scatter(numer, "aux", scatter_dimension=0, tiled=True)
    lower = lax.axis_index("aux") * share
    denom_rows = lax.dynamic_slice_in_dim(denom, lower, share, 0)
    amps_rows = (mine / denom_rows).astype(jnp.bfloat16)
    amps = lax.all_gather(amps_rows, "aux", axis=0, tiled=True)
    return amps


def apply_other(amps, rows_i):
    return lax.dot_general(
        amps, rows_i, (((0,), (0,)), ((), ())), preferred_element_type=jnp.float32
    )


def local(three_index, occ_energy, vir_energy):
    occ_count, vir_count, aux_count = three_index.shape
    cycle_size = lax.axis_size("occ")
    my_index = lax.axis_index("occ")
    all_energy = lax.all_gather(occ_energy, "occ", axis=0, tiled=True)
    own_rows = three_index.reshape(occ_count * vir_count, aux_count)

    def energy_of(step):
        block = (my_index - step + cycle_size) % cycle_size
        return lax.dynamic_slice_in_dim(all_energy, block * occ_count, occ_count)

    amps = pair_amps(own_rows, occ_energy, own_rows, occ_energy, vir_energy)
    gamma = jnp.dot(amps, own_rows, preferred_element_type=jnp.float32)
    half = cycle_size // 2
    carried = jnp.zeros_like(gamma)

    def cycle_step(step, state):
        rows_j, carried, gamma = state
        rows_j = from_behind(rows_j, "occ", 1)
        carried = from_behind(carried, "occ", 1)
        amps = pair_amps(own_rows, occ_energy, rows_j, energy_of(step), vir_energy)
        gamma = gamma + jnp.dot(amps, rows_j, preferred_element_type=jnp.float32)
        carried = carried + apply_other(amps, own_rows)
        return (rows_j, carried, gamma)

    rows_j, carried, gamma = lax.fori_loop(1, half, cycle_step, (own_rows, carried, gamma))
    rows_j = from_behind(rows_j, "occ", 1)
    amps = pair_amps(own_rows, occ_energy, rows_j, energy_of(half), vir_energy)
    gamma = gamma + jnp.dot(amps, rows_j, preferred_element_type=jnp.float32)
    returned = from_behind(carried, "occ", 1 - half)
    gamma = gamma + returned
    return gamma.reshape(occ_count, vir_count, aux_count)


def solution(mesh):
    return jax.shard_map(
        local,
        mesh=mesh,
        in_specs=(P("occ", None, "aux"), P("occ"), P()),
        out_specs=P("occ", None, "aux"),
        check_vma=False,
    )
```

profile of v0, /device:TPU:0, one launch (start us, length us, event | category | flops | bytes accessed | tf_op | source)
XLA Modules:
  0.0 245.2 jit_solution(12605190804021522778)
XLA Ops:
  6.5 1.5 fusion.12
  8.6 1.3 copy.16
  11.9 0.8 dynamic-update-slice
  12.6 23.1 %all-reduce = f32[8]{0:T(128)S(1)} all-reduce(f32[8]{0:T(128)S(1)} %dynamic-update-slice), channel_id=1, replica_groups=mesh['occ'=8,'aux'=4] {'occ'}, use_global_device_ids=true, to_apply=%add | all-reduce | flops 8 | bytes 64
  35.7 0.7 copy.32
  36.5 0.7 copy-done.7
  37.3 1.3 copy.17
  38.9 6.8 %all_gather.19 = bf16[448,448]{1,0:T(8,128)(2,1)S(1)} all-gather(bf16[112,448]{1,0:T(8,128)(2,1)S(1)} %copy.11), channel_id=1, replica_groups=mesh['occ'=8,'aux'=4] {'aux'}, dimensions={0}, use_global_device_ids=true | all-gather | bytes 501760 | tf_op jit(solution)/shard_map/all_gather | solution.py:32
  45.8 1.3 fusion.10
  47.0 143.6 %while.20 = (s32[]{:T(128)}, bf16[448,384]{1,0:T(8,128)(2,1)}, f32[448,384]{1,0:T(8,128)}, f32[448,384]{1,0:T(8,128)}, bf16[448,384]{1,0:T(8,128)(2,1)S(1)}, /*i...) while((s32[]{:T(128)}, bf16[448,384]{1,0:T(8,128)(2,1)}, ...), condition=%wide.region_3.4_spmd.clone, body=%wide.region_1.3_spmd.clone.sunk | while | flops 463590400 | bytes 30367396 | solution.py:67
  47.2 13.1 %collective-permute-done = bf16[448,384]{1,0:T(8,128)(2,1)S(1)} collective-permute-done((bf16[448,384]{1,0:T(8,128)(2,1)}, bf16[448,384]{1,0:T(8,128)(2,1)S(1)}, u32[]{:S(2)}, u32[]{:S(2)}) %collective-permute-start) | collective-permute-done | bytes 344096 | tf_op jit(solution)/shard_map/while/body/eval_jaxpr/ppermute | solution.py:9
  61.2 1.3 copy.27
  62.5 1.1 copy-done.4
  64.4 0.7 copy.40
  65.1 18.4 %reduce-scatter.16.cloned.1.call-done = f32[112,448]{1,0:T(8,128)} async-done(((f32[448,448]{1,0:T(8,128)}), f32[112,448]{1,0:T(8,128)}) %reduce-scatter.16.cloned.1.call-update) | async-done | bytes 200720 | tf_op jit(solution)/shard_map/while
  83.5 1.1 copy.28
  84.6 1.5 fusion.42
  86.2 6.3 %all_gather.24 = bf16[448,448]{1,0:T(8,128)(2,1)S(1)} all-gather(bf16[112,448]{1,0:T(8,128)(2,1)S(1)} %copy.29), channel_id=1, replica_groups=mesh['occ'=8,'aux'=4] {'aux'}, dimensions={0}, use_global_device_ids=true | all-gather | bytes 501760 | tf_op jit(solution)/shard_map/while/body/eval_jaxpr/all_gather | solution.py:32
  93.0 1.3 convolution_add_fusion.5
  94.3 1.5 collective-permute-start
  95.7 11.7 %collective-permute-done = bf16[448,384]{1,0:T(8,128)(2,1)S(1)} collective-permute-done((bf16[448,384]{1,0:T(8,128)(2,1)}, bf16[448,384]{1,0:T(8,128)(2,1)S(1)}, u32[]{:S(2)}, u32[]{:S(2)}) %collective-permute-start) | collective-permute-done | bytes 344096 | tf_op jit(solution)/shard_map/while/body/eval_jaxpr/ppermute | solution.py:9
  108.4 1.3 copy.27
  109.8 1.1 copy-done.4
  111.6 0.7 copy.40
  112.4 19.3 %reduce-scatter.16.cloned.1.call-done = f32[112,448]{1,0:T(8,128)} async-done(((f32[448,448]{1,0:T(8,128)}), f32[112,448]{1,0:T(8,128)}) %reduce-scatter.16.cloned.1.call-update) | async-done | bytes 200720 | tf_op jit(solution)/shard_map/while
  131.7 1.1 copy.28
  132.8 1.5 fusion.42
  134.4 6.3 %all_gather.24 = bf16[448,448]{1,0:T(8,128)(2,1)S(1)} all-gather(bf16[112,448]{1,0:T(8,128)(2,1)S(1)} %copy.29), channel_id=1, replica_groups=mesh['occ'=8,'aux'=4] {'aux'}, dimensions={0}, use_global_device_ids=true | all-gather | bytes 501760 | tf_op jit(solution)/shard_map/while/body/eval_jaxpr/all_gather | solution.py:32
  141.1 1.3 convolution_add_fusion.5
  142.4 1.5 collective-permute-start
  143.9 11.8 %collective-permute-done = bf16[448,384]{1,0:T(8,128)(2,1)S(1)} collective-permute-done((bf16[448,384]{1,0:T(8,128)(2,1)}, bf16[448,384]{1,0:T(8,128)(2,1)S(1)}, u32[]{:S(2)}, u32[]{:S(2)}) %collective-permute-start) | collective-permute-done | bytes 344096 | tf_op jit(solution)/shard_map/while/body/eval_jaxpr/ppermute | solution.py:9
  156.6 1.3 copy.27
  157.9 1.1 copy-done.4
  159.8 0.7 copy.40
  160.5 19.3 %reduce-scatter.16.cloned.1.call-done = f32[112,448]{1,0:T(8,128)} async-done(((f32[448,448]{1,0:T(8,128)}), f32[112,448]{1,0:T(8,128)}) %reduce-scatter.16.cloned.1.call-update) | async-done | bytes 200720 | tf_op jit(solution)/shard_map/while
  179.9 1.1 copy.28
  180.9 1.5 fusion.42
  182.6 6.3 %all_gather.24 = bf16[448,448]{1,0:T(8,128)(2,1)S(1)} all-gather(bf16[112,448]{1,0:T(8,128)(2,1)S(1)} %copy.29), channel_id=1, replica_groups=mesh['occ'=8,'aux'=4] {'aux'}, dimensions={0}, use_global_device_ids=true | all-gather | bytes 501760 | tf_op jit(solution)/shard_map/while/body/eval_jaxpr/all_gather | solution.py:32
  189.3 1.3 convolution_add_fusion.5
  190.6 1.5 collective-permute-start.2
  192.1 11.8 %collective-permute-done.2 = bf16[448,384]{1,0:T(8,128)(2,1)S(1)} collective-permute-done((bf16[448,384]{1,0:T(8,128)(2,1)}, bf16[448,384]{1,0:T(8,128)(2,1)S(1)}, u32[]{:S(2)}, u32[]{:S(2)}) %collective-permute-start.2) | collective-permute-done | bytes 344096 | tf_op jit(solution)/shard_map/ppermute | solution.py:9
  204.8 1.3 copy.18
  206.1 1.1 copy-done.5
  208.4 19.6 %reduce-scatter.14.cloned.1.call-done = f32[112,448]{1,0:T(8,128)} async-done(((f32[448,448]{1,0:T(8,128)}), f32[112,448]{1,0:T(8,128)}) %reduce-scatter.14.cloned.1.call-update) | async-done | bytes 200720
  228.0 1.1 copy.19
  229.1 1.9 fusion.6
  231.1 6.3 %all_gather.21 = bf16[448,448]{1,0:T(8,128)(2,1)S(1)} all-gather(bf16[112,448]{1,0:T(8,128)(2,1)S(1)} %copy.14), channel_id=1, replica_groups=mesh['occ'=8,'aux'=4] {'aux'}, dimensions={0}, use_global_device_ids=true | all-gather | bytes 501760 | tf_op jit(solution)/shard_map/all_gather | solution.py:32
  237.4 1.3 fusion.3
  (82 shorter events, 11.3 us)
Async XLA Ops:
  6.5 30.8 %reduce-scatter.12.cloned.1.call-start = ((), (), s32[]{:S(2)}) async-start(), calls=%async_computation.3 | async-start | bytes 1146880
  9.9 25.8 %copy-start = (bf16[1,448,384]{2,1,0:T(8,128)(2,1)S(1)}, bf16[1,448,384]{2,1,0:T(8,128)(2,1)}, u32[]{:S(2)}) copy-start(bf16[1,448,384]{2,1,0:T(8,128)(2,1)} %param.5) | copy-start | bytes 1032196
  10.6 0.7 copy-start.8
  36.5 0.7 copy-start.7
  37.3 8.5 %copy-start.6 = (f32[1,448,1,448]{1,3,2,0:T(8,128)}, f32[1,448,1,448]{1,3,2,0:T(8,128)S(1)}, u32[]{:S(2)}) copy-start(f32[1,448,1,448]{1,3,2,0:T(8,128)S(1)} %add_subtract_fusion) | copy-start | bytes 2408452
  47.0 36.5 %reduce-scatter.16.cloned.1.call-start = ((), (), s32[]{:S(2)}) async-start(), calls=%async_computation.5 | async-start | bytes 1146880 | tf_op jit(solution)/shard_map/while
  47.0 13.2 %collective-permute-start = (bf16[448,384]{1,0:T(8,128)(2,1)}, bf16[448,384]{1,0:T(8,128)(2,1)S(1)}, u32[]{:S(2)}, u32[]{:S(2)}) collective-permute-start(bf16[448,384]{1,0:T(8,128)(2,1)} %get-tuple-element.351), channel_id=1, source_target_pairs={{0,4},{4,8},{8,12},{12,16},{16,20},{20,24},{24,28},{28,0},{1,5},{5... | collective-permute-start | bytes 1032200 | tf_op jit(solution)/shard_map/while/body/eval_jaxpr/ppermute | solution.py:9
  62.5 1.1 copy-start.4
  63.7 29.3 %collective-permute-start.1 = (f32[448,384]{1,0:T(8,128)S(1)}, f32[448,384]{1,0:T(8,128)S(1)}, u32[]{:S(2)}, u32[]{:S(2)}) collective-permute-start(f32[448,384]{1,0:T(8,128)S(1)} %broadcast_select_fusion.2), channel_id=1, source_target_pairs={{0,4},{4,8},{8,12},{12,16},{16,20},{20,24},{24,28},{28,0},{1,5},{5... | collective-permute-start | bytes 2064392 | tf_op jit(solution)/shard_map/while/body/eval_jaxpr/ppermute | solution.py:9
  84.6 8.0 %copy-start.1 = (f32[448,384]{1,0:T(8,128)S(1)}, f32[448,384]{1,0:T(8,128)}, u32[]{:S(2)}) copy-start(f32[448,384]{1,0:T(8,128)} %get-tuple-element.353) | copy-start | bytes 2064388 | tf_op jit(solution)/shard_map/while
  92.9 1.3 copy-start.2
  94.3 37.4 %reduce-scatter.16.cloned.1.call-start = ((), (), s32[]{:S(2)}) async-start(), calls=%async_computation.5 | async-start | bytes 1146880 | tf_op jit(solution)/shard_map/while
  94.3 13.2 %collective-permute-start = (bf16[448,384]{1,0:T(8,128)(2,1)}, bf16[448,384]{1,0:T(8,128)(2,1)S(1)}, u32[]{:S(2)}, u32[]{:S(2)}) collective-permute-start(bf16[448,384]{1,0:T(8,128)(2,1)} %get-tuple-element.351), channel_id=1, source_target_pairs={{0,4},{4,8},{8,12},{12,16},{16,20},{20,24},{24,28},{28,0},{1,5},{5... | collective-permute-start | bytes 1032200 | tf_op jit(solution)/shard_map/while/body/eval_jaxpr/ppermute | solution.py:9
  109.7 1.1 copy-start.4
  110.9 30.3 %collective-permute-start.1 = (f32[448,384]{1,0:T(8,128)S(1)}, f32[448,384]{1,0:T(8,128)S(1)}, u32[]{:S(2)}, u32[]{:S(2)}) collective-permute-start(f32[448,384]{1,0:T(8,128)S(1)} %broadcast_select_fusion.2), channel_id=1, source_target_pairs={{0,4},{4,8},{8,12},{12,16},{16,20},{20,24},{24,28},{28,0},{1,5},{5... | collective-permute-start | bytes 2064392 | tf_op jit(solution)/shard_map/while/body/eval_jaxpr/ppermute | solution.py:9
  132.8 8.0 %copy-start.1 = (f32[448,384]{1,0:T(8,128)S(1)}, f32[448,384]{1,0:T(8,128)}, u32[]{:S(2)}) copy-start(f32[448,384]{1,0:T(8,128)} %get-tuple-element.353) | copy-start | bytes 2064388 | tf_op jit(solution)/shard_map/while
  141.1 1.3 copy-start.2
  142.4 37.4 %reduce-scatter.16.cloned.1.call-start = ((), (), s32[]{:S(2)}) async-start(), calls=%async_computation.5 | async-start | bytes 1146880 | tf_op jit(solution)/shard_map/while
  142.4 13.2 %collective-permute-start = (bf16[448,384]{1,0:T(8,128)(2,1)}, bf16[448,384]{1,0:T(8,128)(2,1)S(1)}, u32[]{:S(2)}, u32[]{:S(2)}) collective-permute-start(bf16[448,384]{1,0:T(8,128)(2,1)} %get-tuple-element.351), channel_id=1, source_target_pairs={{0,4},{4,8},{8,12},{12,16},{16,20},{20,24},{24,28},{28,0},{1,5},{5... | collective-permute-start | bytes 1032200 | tf_op jit(solution)/shard_map/while/body/eval_jaxpr/ppermute | solution.py:9
  157.9 1.1 copy-start.4
  159.1 30.3 %collective-permute-start.1 = (f32[448,384]{1,0:T(8,128)S(1)}, f32[448,384]{1,0:T(8,128)S(1)}, u32[]{:S(2)}, u32[]{:S(2)}) collective-permute-start(f32[448,384]{1,0:T(8,128)S(1)} %broadcast_select_fusion.2), channel_id=1, source_target_pairs={{0,4},{4,8},{8,12},{12,16},{16,20},{20,24},{24,28},{28,0},{1,5},{5... | collective-permute-start | bytes 2064392 | tf_op jit(solution)/shard_map/while/body/eval_jaxpr/ppermute | solution.py:9
  180.9 8.0 %copy-start.1 = (f32[448,384]{1,0:T(8,128)S(1)}, f32[448,384]{1,0:T(8,128)}, u32[]{:S(2)}) copy-start(f32[448,384]{1,0:T(8,128)} %get-tuple-element.353) | copy-start | bytes 2064388 | tf_op jit(solution)/shard_map/while
  189.3 1.3 copy-start.2
  190.6 37.4 %reduce-scatter.14.cloned.1.call-start = ((), (), s32[]{:S(2)}) async-start(), calls=%async_computation.4 | async-start | bytes 1146880
  190.6 13.2 %collective-permute-start.2 = (bf16[448,384]{1,0:T(8,128)(2,1)}, bf16[448,384]{1,0:T(8,128)(2,1)S(1)}, u32[]{:S(2)}, u32[]{:S(2)}) collective-permute-start(bf16[448,384]{1,0:T(8,128)(2,1)} %get-tuple-element.229), channel_id=1, source_target_pairs={{0,4},{4,8},{8,12},{12,16},{16,20},{20,24},{24,28},{28,0},{1,5},{5... | collective-permute-start | bytes 1032200 | tf_op jit(solution)/shard_map/ppermute | solution.py:9
  206.1 1.1 copy-start.5
  207.2 30.2 %collective-permute-start.3 = (f32[448,384]{1,0:T(8,128)S(1)}, f32[448,384]{1,0:T(8,128)S(1)}, u32[]{:S(2)}, u32[]{:S(2)}) collective-permute-start(f32[448,384]{1,0:T(8,128)S(1)} %copy-done.5), channel_id=1, source_target_pairs={{0,20},{4,24},{8,28},{12,0},{16,4},{20,8},{24,12},{28,16},{1,21},{... | collective-permute-start | bytes 2064392 | tf_op jit(solution)/shard_map/ppermute | solution.py:9
  229.1 8.3 %copy-start.3 = (f32[448,384]{1,0:T(8,128)S(1)}, f32[448,384]{1,0:T(8,128)}, u32[]{:S(2)}) copy-start(f32[448,384]{1,0:T(8,128)} %get-tuple-element.228) | copy-start | bytes 2064388
Sparse Core Ops, SparseCore 0:
  10.0 26.6 reduce-scatter.11
  62.6 20.8 reduce-scatter.15
  109.9 21.7 reduce-scatter.15
  158.0 21.7 reduce-scatter.15
  206.2 21.7 reduce-scatter.13
where the time goes:
time: 246 us; the launch traced here: 245 us
  waiting for transfers between devices  125 us (51%)
  blocking collectives  55.2 us (22%)
  local copies, waits for them, and re-layouts  26.7 us (11%)
  between operations  13.9 us (6%)
  matrix products  10.9 us (4%)
  other arithmetic  7.73 us (3%)
  starting transfers between devices  5.33 us (2%)
    while x6, waiting for transfers between devices  57 us
    ppermute x8, waiting for transfers between devices, from_behind(): lax.ppermute(array, axis, [(i, (i + by) % size) for i in range(size)])  48.3 us
    all_gather x5, blocking collectives, pair_amps(): amps = lax.all_gather(amps_rows, 'aux', axis=0, tiled=True)  32.1 us
    unnamed x1, blocking collectives  23.1 us
    unnamed x4, waiting for transfers between devices  19.7 us
    while x27, local copies, waits for them, and re-layouts  12.5 us
    unnamed x20, local copies, waits for them, and re-layouts  9.47 us
    convert_element_type x5, other arithmetic, pair_amps(): amps_rows = (mine / denom_rows).astype(jnp.bfloat16)  6.5 us
  transfers between devices with their start and end apart: 13, of which 8 were waited for; matrix products, arithmetic and copies ran while one was open for 8% of the time, Pallas kernels for 0%

commit v1 on v0

--- a/solution.py
+++ b/solution.py
@@ -1,12 +1,257 @@
+import functools
+import heapq
+
 import jax
 import jax.numpy as jnp
 from jax import lax
+from jax.experimental import pallas as pl
+from jax.experimental.pallas import tpu as pltpu
 from jax.sharding import PartitionSpec as P
+
+MESH = pl.DeviceIdType.MESH
+CORES = 2
+GATHER_LIMIT = 24 * 1024 * 1024
+PIECES = ((0.5, "xyz"), (0.25, "zyx"), (0.25, "zxy"))
+RATE = {"x": 46.0, "y": 46.0, "z": 46.0, "c": 150.0}
+HOP = {"x": 1700.0, "y": 1700.0, "z": 1700.0, "c": 900.0}
 
 
 def from_behind(array, axis, by):
     size = lax.axis_size(axis)
     return lax.ppermute(array, axis, [(i, (i + by) % size) for i in range(size)])
+
+
+def reach(size):
+    return {1: size // 2, -1: (size - 1) // 2}
+
+
+def piece_rows(rows):
+    pieces, low = [], 0
+    for at, (share, order) in enumerate(PIECES):
+        count = int(rows * share) // 16 * 16
+        if at == len(PIECES) - 1:
+            count = rows - low
+        pieces.append((low, count, order))
+        low += count
+    return pieces
+
+
+def moves(rel, arrived, order, sizes, flip):
+    out = []
+    first = 0
+    if arrived is not None:
+        way = 1 if rel[arrived] > 0 else -1
+        if abs(rel[arrived]) < reach(sizes[arrived])[way]:
+            out.append((arrived, way))
+        first = order.index(arrived) + 1
+    for dim in order[first:]:
+        for way in (1, -1):
+            if reach(sizes[dim])[way] >= 1:
+                out.append((dim, way))
+    return out
+
+
+def plan(rows, width, sizes):
+    pieces = piece_rows(rows)
+    free = {}
+    heap, count = [], 0
+    for at, (_, _, order) in enumerate(pieces):
+        heap.append((0.0, count, at, (0, 0, 0), None, "own"))
+        count += 1
+    heapq.heapify(heap)
+    events = []
+
+    def queue(link, now, size):
+        start = max(now, free.get(link, 0.0))
+        free[link] = start + size / RATE[link[0]]
+        return free[link] + HOP[link[0]]
+
+    while heap:
+        now, _, at, rel, arrived, kind = heapq.heappop(heap)
+        low, number, order = pieces[at]
+        size = number * width * 2
+        if kind == "core":
+            events.append((now, at, rel, "core", ()))
+            continue
+        named = dict(zip("xyz", rel))
+        onward = moves(named, arrived, order, sizes, None)
+        sends = []
+        for dim, way in onward:
+            when = queue((dim, way), now, size)
+            after = dict(named)
+            after[dim] += way
+            heapq.heappush(heap, (when, count, at, (after["x"], after["y"], after["z"]), dim, "link"))
+            count += 1
+            sends.append((dim, way))
+        when = queue(("c", 1), now, size)
+        heapq.heappush(heap, (when, count, at, rel, None, "core"))
+        count += 1
+        events.append((now, at, rel, kind, tuple(sends)))
+    return pieces, events
+
+
+def gather_kernel(nz, nx, ny, b_ref, e_ref, col_ref, row_ref, out_ref, blocks, energies,
+                  send_sem, recv_sem, esend_sem, erecv_sem, own_sem):
+    rows, width = b_ref.shape
+    occ, aux = lax.axis_index("occ"), lax.axis_index("aux")
+    z, x = occ // nx, occ % nx
+    y, core = aux // CORES, aux % CORES
+    sizes = {"x": nx, "y": ny, "z": nz}
+    turn = 1 - 2 * core
+    pieces, events = plan(rows, width, sizes)
+    nocc = nz * nx
+
+    def device(dx, dy, dz, dc):
+        return (
+            ((z + turn * dz + nz) % nz) * nx + (x + dx + nx) % nx,
+            ((y + dy + ny) % ny) * CORES + (core + dc) % CORES,
+        )
+
+    barrier = pltpu.get_barrier_semaphore()
+    for step in range(1, nocc):
+        pl.semaphore_signal(barrier, inc=1, device_id=((occ + step) % nocc, aux), device_id_type=MESH)
+    near = [(occ, (aux // CORES) * CORES + (core + 1) % CORES)]
+    for way in (1, -1):
+        if reach(ny)[way] >= 1:
+            near.append(device(0, way, 0, 0))
+    for target in near:
+        pl.semaphore_signal(barrier, inc=1, device_id=target, device_id_type=MESH)
+    pl.semaphore_wait(barrier, nocc - 1 + len(near))
+
+    def columns(shard_aux):
+        return pl.ds(pl.multiple_of(shard_aux * width, width), width)
+
+    def place(at, shard):
+        low, number, _ = pieces[at]
+        return blocks.at[shard[0], pl.ds(low, number), columns(shard[1])]
+
+    def source(at, shard, own):
+        low, number, _ = pieces[at]
+        return b_ref.at[pl.ds(low, number)] if own else place(at, shard)
+
+    own_copy = pltpu.make_async_copy(b_ref, blocks.at[occ, :, columns(aux)], own_sem)
+    own_copy.start()
+    sent = []
+
+    def send(at, shard, own, target):
+        copy = pltpu.make_async_remote_copy(
+            src_ref=source(at, shard, own), dst_ref=place(at, shard),
+            send_sem=send_sem.at[len(sent)], recv_sem=recv_sem.at[at, shard[0], shard[1]],
+            device_id=target, device_id_type=MESH,
+        )
+        copy.start()
+        sent.append(copy)
+
+    def arrive(at, shard):
+        spot = place(at, shard)
+        pltpu.make_async_remote_copy(
+            src_ref=spot, dst_ref=spot, send_sem=own_sem, recv_sem=recv_sem.at[at, shard[0], shard[1]],
+            device_id=(occ, aux), device_id_type=MESH,
+        ).wait_recv()
+
+    left = {}
+    ready = []
+    for _, at, rel, kind, _ in events:
+        key = (rel[0] % nx, rel[2] % nz)
+        left[key] = left.get(key, 0) + 1
+    waiting = {"energies": True}
+    small = []
+    done = [False]
+
+    def compute(key):
+        block = device(-key[0], 0, -key[1], 0)[0]
+        mine, other = blocks.at[occ], blocks.at[block]
+        value = lax.dot_general(mine[...], other[...], (((1,), (1,)), ((), ())), preferred_element_type=jnp.float32)
+        numer = 2.0 * value - value.T
+        denom = col_ref[...] + row_ref[...] - e_ref[0:1, 0:1] - energies[block, 0:1, 0:1]
+        amps = (numer / denom).astype(jnp.bfloat16)
+        term = jnp.dot(amps, blocks[block, :, columns(aux)], preferred_element_type=jnp.float32)
+        out_ref[...] = out_ref[...] + term if done[0] else term
+        done[0] = True
+
+    started = False
+    for _, at, rel, kind, sends in events:
+        dx, dy, dz = -rel[0], -rel[1], -rel[2]
+        key = (rel[0] % nx, rel[2] % nz)
+        if kind == "core":
+            arrive(at, partner_shard(device, nz, nx, z, x, y, core, turn, dx, dy, dz, ny))
+            rel_key = (rel[0] % nx, (-rel[2]) % nz)
+            key = rel_key
+        else:
+            shard = device(dx, dy, dz, 0)
+            if kind == "link":
+                arrive(at, shard)
+            for dim, way in sends:
+                step = {"x": 0, "y": 0, "z": 0}
+                step[dim] = way
+                send(at, shard, kind == "own", device(step["x"], step["y"], step["z"], 0))
+            send(at, shard, kind == "own", device(0, 0, 0, 1))
+        left[key] -= 1
+        if kind == "own" and not started and at == len(pieces) - 1:
+            started = True
+            keep = pltpu.make_async_copy(e_ref, energies.at[occ], esend_sem.at[0])
+            keep.start()
+            for step in range(1, nocc):
+                copy = pltpu.make_async_remote_copy(
+                    src_ref=e_ref, dst_ref=energies.at[occ], send_sem=esend_sem.at[step],
+                    recv_sem=erecv_sem.at[occ], device_id=((occ + step) % nocc, aux), device_id_type=MESH,
+                )
+                copy.start()
+                small.append(copy)
+            keep.wait()
+            own_copy.wait()
+        if left[key] == 0:
+            left[key] = -1
+            ready.append(key)
+            if (0, 0) in ready or done[0]:
+                for one in ready:
+                    if one != (0, 0) and waiting["energies"]:
+                        waiting["energies"] = False
+                        for step in range(1, nocc):
+                            who = (occ + step) % nocc
+                            pltpu.make_async_remote_copy(
+                                src_ref=e_ref, dst_ref=energies.at[who], send_sem=own_sem,
+                                recv_sem=erecv_sem.at[who], device_id=(occ, aux), device_id_type=MESH,
+                            ).wait_recv()
+                    compute(one)
+                ready.clear()
+    for copy in sent + small:
+        copy.wait_send()
+
+
+def partner_shard(device, nz, nx, z, x, y, core, turn, dx, dy, dz, ny):
+    return (
+        ((z - turn * dz + nz) % nz) * nx + (x + dx + nx) % nx,
+        ((y + dy + ny) % ny) * CORES + (core + 1) % CORES,
+    )
+
+
+def gathered(three_index, occ_energy, vir_energy, nz, nx, ny):
+    _, rows, width = three_index.shape
+    nocc, naux = nz * nx, ny * CORES
+    pieces, events = plan(rows, width, {"x": nx, "y": ny, "z": nz})
+    copies = sum(len(e[4]) + 1 for e in events if e[3] != "core")
+    energy = jnp.broadcast_to(occ_energy.reshape(1, 1), (8, 128))
+    vmem = pl.BlockSpec(memory_space=pltpu.VMEM)
+    out = pl.pallas_call(
+        functools.partial(gather_kernel, nz, nx, ny),
+        out_shape=jax.ShapeDtypeStruct((rows, width), jnp.float32),
+        in_specs=[vmem] * 4,
+        out_specs=vmem,
+        scratch_shapes=[
+            pltpu.VMEM((nocc, rows, naux * width), three_index.dtype),
+            pltpu.VMEM((nocc, 8, 128), jnp.float32),
+            pltpu.SemaphoreType.DMA((copies,)),
+            pltpu.SemaphoreType.DMA((len(pieces), nocc, naux)),
+            pltpu.SemaphoreType.DMA((nocc,)),
+            pltpu.SemaphoreType.DMA((nocc,)),
+            pltpu.SemaphoreType.DMA,
+        ],
+        compiler_params=pltpu.CompilerParams(
+            collective_id=0, has_side_effects=True, vmem_limit_bytes=48 * 1024 * 1024
+        ),
+    )(three_index[0], energy, vir_energy[:, None], vir_energy[None, :])
+    return out[None]
 
 
 def pair_amps(rows_i, eps_i, rows_j, eps_j, vir_energy):
@@ -74,8 +319,18 @@
 
 
 def solution(mesh):
+    nocc, naux = mesh.shape["occ"], mesh.shape["aux"]
+
+    def either(three_index, occ_energy, vir_energy):
+        _, rows, width = three_index.shape
+        whole = nocc * naux * three_index.size * three_index.dtype.itemsize
+        fits = whole <= GATHER_LIMIT and three_index.shape[0] == 1
+        if fits and naux % CORES == 0 and nocc % 2 == 0:
+            return gathered(three_index, occ_energy, vir_energy, nocc // 2, 2, naux // CORES)
+        return local(three_index, occ_energy, vir_energy)
+
     return jax.shard_map(
-        local,
+        either,
         mesh=mesh,
         in_specs=(P("occ", None, "aux"), P("occ"), P()),
         out_specs=P("occ", None, "aux"),

time: 246 us -> 72.5 us (0.29)
  waiting for transfers between devices: 125 us -> 0 us
  Pallas kernels: 0 us -> 69 us
  blocking collectives: 55.2 us -> 0 us
  local copies, waits for them, and re-layouts: 26.7 us -> 2.63 us
  between operations: 13.9 us -> 0.69 us
  matrix products: 10.9 us -> 0 us
  other arithmetic: 7.73 us -> 0 us
  starting transfers between devices: 5.33 us -> 0 us
    pallas_call x0 -> x1, Pallas kernels: none -> 69 us  [gathered(): pl.pallas_call(functools.partial(gather_kernel, nz, nx, ny), out_shape=ja...]
    while x6 -> x0, waiting for transfers between devices: 57 us -> none
    ppermute x8 -> x0, waiting for transfers between devices: 48.3 us -> none  [from_behind(): lax.ppermute(array, axis, [(i, (i + by) % size) for i in range(size)])]
    all_gather x5 -> x0, blocking collectives: 32.1 us -> none  [pair_amps(): amps = lax.all_gather(amps_rows, 'aux', axis=0, tiled=True)]
    unnamed x1 -> x0, blocking collectives: 23.1 us -> none
    unnamed x4 -> x0, waiting for transfers between devices: 19.7 us -> none
    while x27 -> x0, local copies, waits for them, and re-layouts: 12.5 us -> none
    dot_general x13 -> x0, matrix products: 10.9 us -> none  [the longest x3 3.88 us: apply_other(): lax.dot_general(amps, rows_i, (((0,), (0,)), ((), ())), preferred_element...]
  transfers between devices with their start and end apart: 13 -> 0, of which waited for: 8 -> 0; matrix products, arithmetic and copies ran while one was open for 8% -> 0% of each run, Pallas kernels for 0% -> 0%
where the time goes in v1:
time: 72.5 us; the launch traced here: 72.3 us
  Pallas kernels  69 us (95%)
  local copies, waits for them, and re-layouts  2.63 us (4%)
    pallas_call x1, Pallas kernels, gathered(): pl.pallas_call(functools.partial(gather_kernel, nz, nx, ny), out_shape=ja...  69 us
    unnamed x5, local copies, waits for them, and re-layouts  2.49 us

profile of v1, /device:TPU:0, one launch (start us, length us, event | category | flops | bytes accessed | tf_op | source)
XLA Modules:
  0.0 72.3 jit_solution(4254356730465234015)
XLA Ops:
  0.7 0.0 copy-start.1
  0.7 0.7 copy-done.1
  1.3 0.1 copy.4.col_ref
  1.5 0.0 copy-start
  1.5 1.0 %copy-done = bf16[1,448,384]{2,1,0:T(8,128)(2,1)S(1)} copy-done((bf16[1,448,384]{2,1,0:T(8,128)(2,1)S(1)}, bf16[1,448,384]{2,1,0:T(8,128)(2,1)}, u32[]{:S(2)}) %copy-start) | copy-done | bytes 344088
  2.5 69.0 %shard_map.37 = f32[448,384]{1,0:T(8,128)S(1)} custom-call(bf16[448,384]{1,0:T(8,128)(2,1)S(1)} %bitcast.7, f32[8,128]{1,0:T(8,128)S(1)} %broadcast_in_dim.17.e_ref, f32[448,1]{1,0:T(8,128)S(1)} %copy.4.col_ref, f32[1,448]{1,0:T(1,128)S(1)} %bitcast.9), custom_call_target="tpu_custom_call" | custom-call | tf_op jit(solution)/shard_map/pallas_call | solution.py:236
  71.4 0.8 %copy.7 = f32[1,448,384]{2,1,0:T(8,128)} copy(f32[1,448,384]{2,1,0:T(8,128)S(1)} %bitcast.6) | data formatting | bytes 1376256
  (1 shorter events, 0.0 us)
Async XLA Ops:
  0.7 0.7 copy-start.1
  1.5 1.0 %copy-start = (bf16[1,448,384]{2,1,0:T(8,128)(2,1)S(1)}, bf16[1,448,384]{2,1,0:T(8,128)(2,1)}, u32[]{:S(2)}) copy-start(bf16[1,448,384]{2,1,0:T(8,128)(2,1)} %param.3) | copy-start | bytes 1032196

commit v2 on v0

--- a/solution.py
+++ b/solution.py
@@ -1,12 +1,270 @@
+import functools
+import heapq
+import itertools
+
 import jax
 import jax.numpy as jnp
 from jax import lax
+from jax.experimental import pallas as pl
+from jax.experimental.pallas import tpu as pltpu
 from jax.sharding import PartitionSpec as P
+
+MESH = pl.DeviceIdType.MESH
+CORES = 2
+GATHER_LIMIT = 24 * 1024 * 1024
+PIECES = ((0.393, "zyx"), (0.393, "zxy"), (0.214, "xyz"))
+RATE = 90.0
+HOP = 1650.0
+ROUNDS = 6
 
 
 def from_behind(array, axis, by):
     size = lax.axis_size(axis)
     return lax.ppermute(array, axis, [(i, (i + by) % size) for i in range(size)])
+
+
+def piece_rows(rows):
+    pieces, low = [], 0
+    for at, (share, order) in enumerate(PIECES):
+        last = at == len(PIECES) - 1
+        count = rows - low if last else int(rows * share) // 16 * 16
+        pieces.append((low, count, order))
+        low += count
+    return pieces
+
+
+def onward(order, event, sizes):
+    _, dx, dy, dz = event
+    came = {"x": dx, "y": dy, "z": dz}
+    moved = [dim for dim in order if came[dim] != 0]
+    pairs, first = [], 0
+    if moved:
+        first = order.index(moved[-1]) + 1
+        if moved[-1] == "z":
+            pairs.append(("z", -1 if dz > 0 else 1))
+    for dim in order[first:]:
+        if sizes[dim] > 1:
+            pairs.extend([("z", 1), ("z", -1)] if dim == "z" else [(dim, 1)])
+    return pairs
+
+
+def timed(pieces, events, sizes, row_bytes):
+    nx, ny, nz = sizes["x"], sizes["y"], sizes["z"]
+    chips = list(itertools.product(range(nz), range(nx), range(ny)))
+
+    def home(chip, event):
+        return (chip[0] + event[3], (chip[1] + event[1]) % nx, (chip[2] + event[2]) % ny)
+
+    def beside(chip, dim, way):
+        z, x, y = chip
+        return {"z": (z + way, x, y), "x": (z, (x + way) % nx, y), "y": (z, x, (y + way) % ny)}[dim]
+
+    todo = {c: [e for e in events if 0 <= c[0] + e[3] < nz] for c in chips}
+    at_place = {c: 0 for c in chips}
+    arrived = {c: {} for c in chips}
+    free, heap, ticket = {}, [], itertools.count()
+
+    def advance(chip, now):
+        while at_place[chip] < len(todo[chip]):
+            event = todo[chip][at_place[chip]]
+            key = (event[0], home(chip, event))
+            if key[1] != chip and key not in arrived[chip]:
+                return
+            at_place[chip] += 1
+            _, count, order = pieces[event[0]]
+            for dim, way in onward(order, event, sizes):
+                target = beside(chip, dim, way)
+                if 0 <= target[0] < nz:
+                    sent = max(now, free.get((chip, target), 0.0)) + CORES * count * row_bytes / RATE
+                    free[chip, target] = sent
+                    heapq.heappush(heap, (sent + HOP, next(ticket), target, key))
+
+    for chip in chips:
+        advance(chip, 0.0)
+    end = 0.0
+    while heap:
+        end, _, chip, key = heapq.heappop(heap)
+        arrived[chip][key] = end
+        advance(chip, end)
+    times = []
+    for event in events:
+        seen = [arrived[c].get((event[0], home(c, event)), 0.0) for c in chips if 0 <= c[0] + event[3] < nz]
+        times.append((sum(seen) / len(seen) + max(seen)) / 2)
+    return end, times
+
+
+def plan(rows, width, sizes):
+    pieces = piece_rows(rows)
+    span = range(1 - sizes["z"], sizes["z"])
+    events = [
+        (at, dx, dy, dz)
+        for at in range(len(pieces)) for dz in span
+        for dx in range(sizes["x"]) for dy in range(sizes["y"])
+    ]
+    events.sort(key=lambda e: (e[1] + e[2] + abs(e[3]), e[0]))
+    best = None
+    for _ in range(ROUNDS):
+        end, times = timed(pieces, events, sizes, width * 2)
+        if best is None or end < best[0]:
+            best = (end, list(events))
+        order = sorted(range(len(events)), key=lambda k: times[k])
+        events = [events[k] for k in order]
+    return pieces, best[1]
+
+
+def gather_kernel(nz, nx, ny, b_ref, e_ref, col_ref, row_ref, out_ref, blocks, energies,
+                  send_sem, recv_sem, esend_sem, erecv_sem, own_sem):
+    rows, width = b_ref.shape
+    occ, aux = lax.axis_index("occ"), lax.axis_index("aux")
+    z, x = occ // nx, occ % nx
+    y, core = aux // CORES, aux % CORES
+    sizes = {"x": nx, "y": ny, "z": nz}
+    pieces, events = plan(rows, width, sizes)
+    nocc = nz * nx
+
+    def device(dx, dy, dz, dc):
+        return ((z + dz) * nx + lax.rem(x + dx, nx), lax.rem(y + dy, ny) * CORES + lax.rem(core + dc, CORES))
+
+    def inside(dz):
+        return jnp.logical_and(z + dz >= 0, z + dz < nz)
+
+    def when(dz, body):
+        if dz == 0:
+            body()
+        else:
+            pl.when(inside(dz))(body)
+
+    barrier = pltpu.get_barrier_semaphore()
+    peers = [((occ + step) % nocc, aux) for step in range(1, nocc)]
+    near = peers + [device(0, 0, 0, 1)] + ([device(0, 1, 0, 0)] if ny > 1 else [])
+    for target in near:
+        pl.semaphore_signal(barrier, inc=1, device_id=target, device_id_type=MESH)
+
+    def columns(shard_aux):
+        return pl.ds(pl.multiple_of(shard_aux * width, width), width)
+
+    own_copy = pltpu.make_async_copy(b_ref, blocks.at[occ, :, columns(aux)], own_sem)
+    own_copy.start()
+    keep = pltpu.make_async_copy(e_ref, energies.at[occ], esend_sem.at[0])
+    keep.start()
+    out_ref[...] = jnp.zeros_like(out_ref)
+    pl.semaphore_wait(barrier, len(near))
+
+    def place(at, shard):
+        low, number, _ = pieces[at]
+        return blocks.at[shard[0], pl.ds(low, number), columns(shard[1])]
+
+    ends = []
+
+    def send(at, event, shard, target, reached):
+        low, number, _ = pieces[at]
+        own = event[1:] == (0, 0, 0)
+        slot = len(ends)
+
+        def copy():
+            return pltpu.make_async_remote_copy(
+                src_ref=b_ref.at[pl.ds(low, number)] if own else place(at, shard),
+                dst_ref=place(at, shard), send_sem=send_sem.at[slot],
+                recv_sem=recv_sem.at[at, shard[0], shard[1]], device_id=target, device_id_type=MESH,
+            )
+
+        when(reached, lambda: copy().start())
+        ends.append((event[3], reached, lambda: copy().wait_send()))
+
+    def arrive(at, shard):
+        spot = place(at, shard)
+        pltpu.make_async_remote_copy(
+            src_ref=spot, dst_ref=spot, send_sem=own_sem, recv_sem=recv_sem.at[at, shard[0], shard[1]],
+            device_id=(occ, aux), device_id_type=MESH,
+        ).wait_recv()
+
+    def compute(dx, dz):
+        block = device(dx, 0, dz, 0)[0]
+        for at in range(len(pieces)):
+            for dy in range(ny):
+                arrive(at, device(dx, dy, dz, 1))
+        value = lax.dot_general(
+            blocks[occ], blocks[block], (((1,), (1,)), ((), ())), preferred_element_type=jnp.float32
+        )
+        numer = 2.0 * value - value.T
+        denom = col_ref[...] + row_ref[...] - e_ref[0:1, 0:1] - energies[block, 0:1, 0:1]
+        amps = (numer / denom).astype(jnp.bfloat16)
+        out_ref[...] += jnp.dot(amps, blocks[block, :, columns(aux)], preferred_element_type=jnp.float32)
+
+    left = {}
+    for event in events:
+        left[event[1], event[3]] = left.get((event[1], event[3]), 0) + 1
+    full, small, held = False, [], []
+    for event in events:
+        at, dx, dy, dz = event
+        shard = device(dx, dy, dz, 0)
+
+        steps = [{"x": 0, "y": 0, "z": 0, dim: way} for dim, way in onward(pieces[at][2], event, sizes)]
+        targets = [(device(o["x"], o["y"], o["z"], 0), o["z"]) for o in steps] + [(device(0, 0, 0, 1), 0)]
+
+        def pass_on(at=at, event=event, shard=shard, targets=targets):
+            if event[1:] != (0, 0, 0):
+                arrive(at, shard)
+            for target, reached in targets:
+                send(at, event, shard, target, reached)
+
+        when(dz, pass_on)
+        left[dx, dz] -= 1
+        if left[dx, dz] == 0:
+            held.append((dx, dz))
+        if (0, 0) in held and not full:
+            full = True
+            for step, target in enumerate(peers, 1):
+                copy = pltpu.make_async_remote_copy(
+                    src_ref=e_ref, dst_ref=energies.at[occ], send_sem=esend_sem.at[step],
+                    recv_sem=erecv_sem.at[occ], device_id=target, device_id_type=MESH,
+                )
+                copy.start()
+                small.append(copy)
+            keep.wait()
+            own_copy.wait()
+            for who, _ in peers:
+                pltpu.make_async_remote_copy(
+                    src_ref=e_ref, dst_ref=energies.at[who], send_sem=own_sem,
+                    recv_sem=erecv_sem.at[who], device_id=(occ, aux), device_id_type=MESH,
+                ).wait_recv()
+        if full:
+            for one in held:
+                when(one[1], functools.partial(compute, *one))
+            held = []
+    for copy in small:
+        copy.wait_send()
+    for came, reached, wait in ends:
+        when(came, functools.partial(when, reached, wait))
+
+
+def gathered(three_index, occ_energy, vir_energy, nz, nx, ny):
+    _, rows, width = three_index.shape
+    nocc, naux = nz * nx, ny * CORES
+    sizes = {"x": nx, "y": ny, "z": nz}
+    pieces, events = plan(rows, width, sizes)
+    copies = sum(len(onward(pieces[e[0]][2], e, sizes)) + 1 for e in events)
+    energy = jnp.broadcast_to(occ_energy.reshape(1, 1), (8, 128))
+    vmem = pl.BlockSpec(memory_space=pltpu.VMEM)
+    out = pl.pallas_call(
+        functools.partial(gather_kernel, nz, nx, ny),
+        out_shape=jax.ShapeDtypeStruct((rows, width), jnp.float32),
+        in_specs=[vmem] * 4,
+        out_specs=vmem,
+        scratch_shapes=[
+            pltpu.VMEM((nocc, rows, naux * width), three_index.dtype),
+            pltpu.VMEM((nocc, 8, 128), jnp.float32),
+            pltpu.SemaphoreType.DMA((copies,)),
+            pltpu.SemaphoreType.DMA((len(pieces), nocc, naux)),
+            pltpu.SemaphoreType.DMA((nocc,)),
+            pltpu.SemaphoreType.DMA((nocc,)),
+            pltpu.SemaphoreType.DMA,
+        ],
+        compiler_params=pltpu.CompilerParams(
+            collective_id=0, has_side_effects=True, vmem_limit_bytes=48 * 1024 * 1024
+        ),
+    )(three_index[0], energy, vir_energy[:, None], vir_energy[None, :])
+    return out[None]
 
 
 def pair_amps(rows_i, eps_i, rows_j, eps_j, vir_energy):
@@ -74,8 +332,19 @@
 
 
 def solution(mesh):
+    nocc, naux = mesh.shape["occ"], mesh.shape["aux"]
+    pairs = 2 if nocc % 2 == 0 else 1
+
+    def either(three_index, occ_energy, vir_energy):
+        held, rows, width = three_index.shape
+        whole = nocc * naux * three_index.size * three_index.dtype.itemsize
+        even = held == 1 and rows % 16 == 0 and width % 128 == 0
+        if whole <= GATHER_LIMIT and even and naux in (CORES, 2 * CORES):
+            return gathered(three_index, occ_energy, vir_energy, nocc // pairs, pairs, naux // CORES)
+        return local(three_index, occ_energy, vir_energy)
+
     return jax.shard_map(
-        local,
+        either,
         mesh=mesh,
         in_specs=(P("occ", None, "aux"), P("occ"), P()),
         out_specs=P("occ", None, "aux"),

time: 246 us -> 67.8 us (0.28)
  waiting for transfers between devices: 125 us -> 0 us
  Pallas kernels: 0 us -> 64.3 us
  blocking collectives: 55.2 us -> 0 us
  local copies, waits for them, and re-layouts: 26.7 us -> 2.63 us
  between operations: 13.9 us -> 0.69 us
  matrix products: 10.9 us -> 0 us
  other arithmetic: 7.73 us -> 0 us
  starting transfers between devices: 5.33 us -> 0 us
    pallas_call x0 -> x1, Pallas kernels: none -> 64.3 us  [gathered(): pl.pallas_call(functools.partial(gather_kernel, nz, nx, ny), out_shape=ja...]
    while x6 -> x0, waiting for transfers between devices: 57 us -> none
    ppermute x8 -> x0, waiting for transfers between devices: 48.3 us -> none  [from_behind(): lax.ppermute(array, axis, [(i, (i + by) % size) for i in range(size)])]
    all_gather x5 -> x0, blocking collectives: 32.1 us -> none  [pair_amps(): amps = lax.all_gather(amps_rows, 'aux', axis=0, tiled=True)]
    unnamed x1 -> x0, blocking collectives: 23.1 us -> none
    unnamed x4 -> x0, waiting for transfers between devices: 19.7 us -> none
    while x27 -> x0, local copies, waits for them, and re-layouts: 12.5 us -> none
    dot_general x13 -> x0, matrix products: 10.9 us -> none  [the longest x3 3.88 us: apply_other(): lax.dot_general(amps, rows_i, (((0,), (0,)), ((), ())), preferred_element...]
  transfers between devices with their start and end apart: 13 -> 0, of which waited for: 8 -> 0; matrix products, arithmetic and copies ran while one was open for 8% -> 0% of each run, Pallas kernels for 0% -> 0%
where the time goes in v2:
time: 67.8 us; the launch traced here: 67.6 us
  Pallas kernels  64.3 us (95%)
  local copies, waits for them, and re-layouts  2.63 us (4%)
  between operations  0.69 us (1%)
    pallas_call x1, Pallas kernels, gathered(): pl.pallas_call(functools.partial(gather_kernel, nz, nx, ny), out_shape=ja...  64.3 us
    unnamed x5, local copies, waits for them, and re-layouts  2.49 us

profile of v2, /device:TPU:0, one launch (start us, length us, event | category | flops | bytes accessed | tf_op | source)
XLA Modules:
  0.0 67.6 jit_solution(3295051399950948997)
XLA Ops:
  0.7 0.0 copy-start.1
  0.7 0.7 copy-done.1
  1.3 0.1 copy.4.col_ref
  1.5 0.0 copy-start
  1.5 1.0 %copy-done = bf16[1,448,384]{2,1,0:T(8,128)(2,1)S(1)} copy-done((bf16[1,448,384]{2,1,0:T(8,128)(2,1)S(1)}, bf16[1,448,384]{2,1,0:T(8,128)(2,1)}, u32[]{:S(2)}) %copy-start) | copy-done | bytes 344088
  2.5 64.3 %shard_map.37 = f32[448,384]{1,0:T(8,128)S(1)} custom-call(bf16[448,384]{1,0:T(8,128)(2,1)S(1)} %bitcast.7, f32[8,128]{1,0:T(8,128)S(1)} %broadcast_in_dim.17.e_ref, f32[448,1]{1,0:T(8,128)S(1)} %copy.4.col_ref, f32[1,448]{1,0:T(1,128)S(1)} %bitcast.9), custom_call_target="tpu_custom_call" | custom-call | tf_op jit(solution)/shard_map/pallas_call | solution.py:249
  66.7 0.8 %copy.7 = f32[1,448,384]{2,1,0:T(8,128)} copy(f32[1,448,384]{2,1,0:T(8,128)S(1)} %bitcast.6) | data formatting | bytes 1376256
  (1 shorter events, 0.0 us)
Async XLA Ops:
  0.7 0.7 %copy-start.1 = (f32[448]{0:T(512)S(1)}, f32[448]{0:T(512)}, u32[]{:S(2)}) copy-start(f32[448]{0:T(512)} %param.5) | copy-start | bytes 5380
  1.5 1.0 %copy-start = (bf16[1,448,384]{2,1,0:T(8,128)(2,1)S(1)}, bf16[1,448,384]{2,1,0:T(8,128)(2,1)}, u32[]{:S(2)}) copy-start(bf16[1,448,384]{2,1,0:T(8,128)(2,1)} %param.3) | copy-start | bytes 1032196

commit v3 on v1

--- a/solution.py
+++ b/solution.py
@@ -11,8 +11,8 @@
 MESH = pl.DeviceIdType.MESH
 CORES = 2
 GATHER_LIMIT = 24 * 1024 * 1024
-PIECES = ((0.5, "xyz"), (0.25, "zyx"), (0.25, "zxy"))
-RATE = {"x": 46.0, "y": 46.0, "z": 46.0, "c": 150.0}
+PIECES = ((0.145, "yxz"), (0.43, "zyx"), (0.43, "zxy"))
+RATE = {"x": 46.0, "y": 46.0, "z": 25.0, "c": 150.0}
 HOP = {"x": 1700.0, "y": 1700.0, "z": 1700.0, "c": 900.0}
 
 

time: 72.5 us -> 58.9 us (0.81); the launches traced: 72.3 us -> 57.8 us
  Pallas kernels: 69 us -> 54.5 us
    pallas_call x1, Pallas kernels: 69 us -> 54.5 us  [gathered(): pl.pallas_call(functools.partial(gather_kernel, nz, nx, ny), out_shape=ja...]
where the time goes in v3:
time: 58.9 us; the launch traced here: 57.8 us
  Pallas kernels  54.5 us (93%)
  local copies, waits for them, and re-layouts  2.63 us (4%)
  between operations  0.69 us (1%)
    pallas_call x1, Pallas kernels, gathered(): pl.pallas_call(functools.partial(gather_kernel, nz, nx, ny), out_shape=ja...  54.5 us
    unnamed x5, local copies, waits for them, and re-layouts  2.49 us

profile of v3, /device:TPU:0, one launch (start us, length us, event | category | flops | bytes accessed | tf_op | source)
XLA Modules:
  0.0 57.8 jit_solution(6347712836283789635)
XLA Ops:
  0.7 0.0 copy-start.1
  0.7 0.7 %copy-done.1 = f32[448]{0:T(512)S(1)} copy-done((f32[448]{0:T(512)S(1)}, f32[448]{0:T(512)}, u32[]{:S(2)}) %copy-start.1) | copy-done | bytes 1816
  1.3 0.1 copy.4.col_ref
  1.5 0.0 copy-start
  1.5 1.0 %copy-done = bf16[1,448,384]{2,1,0:T(8,128)(2,1)S(1)} copy-done((bf16[1,448,384]{2,1,0:T(8,128)(2,1)S(1)}, bf16[1,448,384]{2,1,0:T(8,128)(2,1)}, u32[]{:S(2)}) %copy-start) | copy-done | bytes 344088
  2.5 54.5 %shard_map.37 = f32[448,384]{1,0:T(8,128)S(1)} custom-call(bf16[448,384]{1,0:T(8,128)(2,1)S(1)} %bitcast.7, f32[8,128]{1,0:T(8,128)S(1)} %broadcast_in_dim.17.e_ref, f32[448,1]{1,0:T(8,128)S(1)} %copy.4.col_ref, f32[1,448]{1,0:T(1,128)S(1)} %bitcast.9), custom_call_target="tpu_custom_call" | custom-call | tf_op jit(solution)/shard_map/pallas_call | solution.py:236
  57.0 0.8 %copy.7 = f32[1,448,384]{2,1,0:T(8,128)} copy(f32[1,448,384]{2,1,0:T(8,128)S(1)} %bitcast.6) | data formatting | bytes 1376256
  (1 shorter events, 0.0 us)
Async XLA Ops:
  0.7 0.7 %copy-start.1 = (f32[448]{0:T(512)S(1)}, f32[448]{0:T(512)}, u32[]{:S(2)}) copy-start(f32[448]{0:T(512)} %param.5) | copy-start | bytes 5380
  1.5 1.0 %copy-start = (bf16[1,448,384]{2,1,0:T(8,128)(2,1)S(1)}, bf16[1,448,384]{2,1,0:T(8,128)(2,1)}, u32[]{:S(2)}) copy-start(bf16[1,448,384]{2,1,0:T(8,128)(2,1)} %param.3) | copy-start | bytes 1032196

commit v4 on v3

--- a/solution.py
+++ b/solution.py
@@ -11,9 +11,9 @@
 MESH = pl.DeviceIdType.MESH
 CORES = 2
 GATHER_LIMIT = 24 * 1024 * 1024
-PIECES = ((0.145, "yxz"), (0.43, "zyx"), (0.43, "zxy"))
+PIECES = ((0.11, "xyz"), (0.445, "zyx"), (0.445, "zxy"))
 RATE = {"x": 46.0, "y": 46.0, "z": 25.0, "c": 150.0}
-HOP = {"x": 1700.0, "y": 1700.0, "z": 1700.0, "c": 900.0}
+HOP = {"x": 1700.0, "y": 1700.0, "z": 3500.0, "c": 900.0}
 
 
 def from_behind(array, axis, by):

time: 58.9 us -> 61.2 us (1.039); the launches traced: 57.8 us -> 61 us
  Pallas kernels: 54.5 us -> 57.7 us
    pallas_call x1, Pallas kernels: 54.5 us -> 57.7 us  [gathered(): pl.pallas_call(functools.partial(gather_kernel, nz, nx, ny), out_shape=ja...]
where the time goes in v4:
time: 61.2 us; the launch traced here: 61 us
  Pallas kernels  57.7 us (94%)
  local copies, waits for them, and re-layouts  2.63 us (4%)
  between operations  0.69 us (1%)
    pallas_call x1, Pallas kernels, gathered(): pl.pallas_call(functools.partial(gather_kernel, nz, nx, ny), out_shape=ja...  57.7 us
    unnamed x5, local copies, waits for them, and re-layouts  2.49 us

profile of v4, /device:TPU:0, one launch (start us, length us, event | category | flops | bytes accessed | tf_op | source)
XLA Modules:
  0.0 61.0 jit_solution(2373309358826257204)
XLA Ops:
  0.7 0.0 copy-start.1
  0.7 0.7 %copy-done.1 = f32[448]{0:T(512)S(1)} copy-done((f32[448]{0:T(512)S(1)}, f32[448]{0:T(512)}, u32[]{:S(2)}) %copy-start.1) | copy-done | bytes 1816
  1.3 0.1 copy.4.col_ref
  1.5 0.0 copy-start
  1.5 1.0 %copy-done = bf16[1,448,384]{2,1,0:T(8,128)(2,1)S(1)} copy-done((bf16[1,448,384]{2,1,0:T(8,128)(2,1)S(1)}, bf16[1,448,384]{2,1,0:T(8,128)(2,1)}, u32[]{:S(2)}) %copy-start) | copy-done | bytes 344088
  2.5 57.7 %shard_map.37 = f32[448,384]{1,0:T(8,128)S(1)} custom-call(bf16[448,384]{1,0:T(8,128)(2,1)S(1)} %bitcast.7, f32[8,128]{1,0:T(8,128)S(1)} %broadcast_in_dim.17.e_ref, f32[448,1]{1,0:T(8,128)S(1)} %copy.4.col_ref, f32[1,448]{1,0:T(1,128)S(1)} %bitcast.9), custom_call_target="tpu_custom_call" | custom-call | tf_op jit(solution)/shard_map/pallas_call | solution.py:236
  60.2 0.8 %copy.7 = f32[1,448,384]{2,1,0:T(8,128)} copy(f32[1,448,384]{2,1,0:T(8,128)S(1)} %bitcast.6) | data formatting | bytes 1376256
  (1 shorter events, 0.0 us)
Async XLA Ops:
  0.7 0.7 %copy-start.1 = (f32[448]{0:T(512)S(1)}, f32[448]{0:T(512)}, u32[]{:S(2)}) copy-start(f32[448]{0:T(512)} %param.5) | copy-start | bytes 5380
  1.5 1.0 %copy-start = (bf16[1,448,384]{2,1,0:T(8,128)(2,1)S(1)}, bf16[1,448,384]{2,1,0:T(8,128)(2,1)}, u32[]{:S(2)}) copy-start(bf16[1,448,384]{2,1,0:T(8,128)(2,1)} %param.3) | copy-start | bytes 1032196
